TPU v7x, 512 devices: a whole 4x8x8 slice. The times are simulated.
512 devices in a mesh: stn: 16 (over z, core), chan: 32 (over y, x).
Axes of the slice: x: 4, y: 8, z: 8, core: 2. Of those that a mesh axis runs over, the one named last changes fastest.
Arguments:
- voltages: bfloat16 [256, 2048, 512], P('stn', 'chan'), may hold values from -6 to 6
- block_facet: int32 [32, 16, 2048, 1], P('chan', 'stn'), may hold values from 0 to 15; in each aligned block of 2048 rows (0 to 2047, 2048 to 4095, ..., all dimensions but the last counted through in order) at most 192 rows name the same one
- block_tile: int32 [32, 16, 2048], P('chan', 'stn'), may hold values from 0 to 15
- vis_offset: int32 [32, 16, 2048, 128], P('chan', 'stn'), may hold values from 0 to 624
- kernel_taps: bfloat16 [2, 8], replicated, may hold values from 0.19921875 to 1
Outputs:
- image: float32 [2, 2048, 128], P(None, ('stn', 'chan'))
Inputs may be any that keep to these rules, and one draw needn't show every extreme that they name: `block_facet`: among the blocks of one device (one index of the first two dimensions) at most 192 name one facet; in every draw some facet is named by exactly 192 of some device's blocks.
All inputs are finite; a program needn't handle non-finite values.
Results may differ from a plain program's by a relative error of at most 0.0041.
Values may be sent and summed in bfloat16 or wider, within the bound.
A program may use at most 64 MiB of HBM per device.

v0:
```python
import math
import jax
import jax.numpy as jnp
from jax import lax
from jax.sharding import PartitionSpec as P

VB = 128
TILE = 32
KT = 8
TS = 4
TT = 16
OFFS = 25


def kernel_rows(offsets, taps_row):
    cell_ids = jnp.arange(TILE, dtype=jnp.int32)
    distance = cell_ids[None, :, None] - offsets[:, None, :]
    weights_sum = jnp.zeros(distance.shape, jnp.float32)
    for tap_index in range(KT):
        weights_sum = weights_sum + jnp.where(
            distance == tap_index, taps_row[tap_index].astype(jnp.float32), jnp.float32(0.0)
        )
    return weights_sum.astype(jnp.bfloat16)


def block_tiles(values, offsets, kernel_taps):
    along_u = kernel_rows(offsets // OFFS, kernel_taps[0])
    along_v = kernel_rows(offsets % OFFS, kernel_taps[1])
    weighted = (
        values[:, :, None, :].astype(jnp.float32) * along_v[:, None, :, :].astype(jnp.float32)
    ).astype(jnp.bfloat16)
    weighted = weighted.reshape(values.shape[0], 2 * TILE, values.shape[2])
    return jnp.einsum("nux,nwx->nuw", along_u, weighted, preferred_element_type=jnp.float32)


def grid_blocks(values, offsets, target_ids, kernel_taps, segments):
    slot_count = values.shape[0]
    group_size = math.gcd(slot_count, 256)
    tile_width = 2 * TILE * TILE
    segment_ids = jnp.arange(segments, dtype=jnp.int32)

    def accumulate(grids, turn_index):
        first_row = turn_index * group_size
        part_values = lax.dynamic_slice_in_dim(values, first_row, group_size, 0)
        part_offsets = lax.dynamic_slice_in_dim(offsets, first_row, group_size, 0)
        part_targets = lax.dynamic_slice_in_dim(target_ids, first_row, group_size, 0)
        tile_sums = block_tiles(part_values, part_offsets, kernel_taps).reshape(
            group_size, tile_width
        )
        placing = (segment_ids[:, None] == part_targets[None, :]).astype(jnp.float32)
        grids = grids + jnp.dot(
            placing, tile_sums, precision=lax.Precision.HIGHEST, preferred_element_type=jnp.float32
        )
        return (grids, None)

    start_grids = jnp.zeros((segments, tile_width), jnp.float32)
    grids, leftover = lax.scan(accumulate, start_grids, jnp.arange(slot_count // group_size))
    return grids


def facet_grid(tile_grid):
    shaped = tile_grid.reshape(TS, TS, TILE, 2, TILE)
    return jnp.transpose(shaped, (3, 0, 2, 1, 4)).reshape(2, TS * TILE, TS * TILE)


def dft_tables(side):
    index_ids = jnp.arange(side, dtype=jnp.int32)
    phases = index_ids[:, None] * index_ids[None, :] % side
    angles = phases.astype(jnp.float32) * (2.0 * math.pi / side)
    return (jnp.cos(angles), jnp.sin(angles))


def column_pass(grid, cosine, sine):
    high = lax.Precision.HIGHEST
    real_cols = jnp.dot(grid[0], cosine, precision=high) + jnp.dot(grid[1], sine, precision=high)
    imag_cols = jnp.dot(grid[1], cosine, precision=high) - jnp.dot(grid[0], sine, precision=high)
    return (real_cols, imag_cols)


def row_pass(real_cols, imag_cols, cosine_rows, sine_rows):
    high = lax.Precision.HIGHEST
    real_rows = jnp.dot(cosine_rows, real_cols, precision=high) + jnp.dot(
        sine_rows, imag_cols, precision=high
    )
    imag_rows = jnp.dot(cosine_rows, imag_cols, precision=high) - jnp.dot(
        sine_rows, real_cols, precision=high
    )
    return (real_rows, imag_rows)


def body(voltages, block_facet, block_tile, vis_offset, kernel_taps):
    facets = lax.axis_size("stn")
    chan_count = lax.axis_size("chan")
    panels = lax.all_to_all(voltages, "stn", split_axis=1, concat_axis=0, tiled=True)
    stations = panels.shape[0]
    local_channels = panels.shape[1]
    samples = panels.shape[2] // 2
    swapped = jnp.concatenate([panels[:, :, samples:], -panels[:, :, :samples]], axis=2)
    stacked = jnp.concatenate([panels, swapped], axis=0)
    products = jnp.einsum("aks,jks->kaj", stacked, panels, preferred_element_type=jnp.float32)
    station_ids = jnp.arange(stations, dtype=jnp.int32)
    off_diagonal = (station_ids[:, None] != station_ids[None, :]).astype(jnp.float32)
    scale = 1.0 / math.sqrt(samples)
    real_vis = (products[:, :stations, :] * scale * off_diagonal).astype(jnp.bfloat16)
    imag_vis = (products[:, stations:, :] * scale * off_diagonal).astype(jnp.bfloat16)
    block_values = jnp.stack([real_vis.reshape(-1, VB), imag_vis.reshape(-1, VB)], axis=1)
    block_count = block_values.shape[0]
    offsets = vis_offset.reshape(block_count, VB)
    tile_ids = block_tile.reshape(block_count)
    facet_ids = block_facet.reshape(block_count)
    capacity = 3 * block_count // (2 * facets)
    facet_range = jnp.arange(facets, dtype=jnp.int32)
    member = (facet_ids[:, None] == facet_range[None, :]).astype(jnp.int32)
    earlier = jnp.cumsum(member, axis=0) - member
    position = jnp.sum(earlier * member, axis=1)
    slot_ids = facet_ids * capacity + position
    send_values = jnp.zeros((facets * capacity, 2, VB), jnp.bfloat16).at[slot_ids].set(block_values)
    send_offsets = jnp.zeros((facets * capacity, VB), jnp.int32).at[slot_ids].set(offsets)
    send_tiles = jnp.zeros((facets * capacity,), jnp.int32).at[slot_ids].set(tile_ids)
    got_values, got_offsets, got_tiles = (
        lax.all_to_all(send_values, "stn", split_axis=0, concat_axis=0, tiled=True),
        lax.all_to_all(send_offsets, "stn", split_axis=0, concat_axis=0, tiled=True),
        lax.all_to_all(send_tiles, "stn", split_axis=0, concat_axis=0, tiled=True),
    )
    tile_grid = grid_blocks(got_values, got_offsets, got_tiles, kernel_taps, TT)
    grid = facet_grid(tile_grid)
    side = grid.shape[1]
    row_count = side // chan_count
    channels_all = local_channels * facets * chan_count
    norm_factor = 1.0 / math.sqrt(channels_all * stations * stations * KT * KT / facets)
    cosine, sine = dft_tables(side)
    summed = lax.psum(grid, "chan")
    real_cols, imag_cols = column_pass(summed, cosine, sine)
    first_row = lax.axis_index("chan") * row_count
    cosine_rows = lax.dynamic_slice_in_dim(cosine, first_row, row_count, 0)
    sine_rows = lax.dynamic_slice_in_dim(sine, first_row, row_count, 0)
    real_rows, imag_rows = row_pass(real_cols, imag_cols, cosine_rows, sine_rows)
    image = jnp.stack([real_rows, imag_rows], axis=0) * norm_factor
    return image


def solution(mesh):
    placed = (
        P("stn", "chan", None),
        P("chan", "stn", None, None),
        P("chan", "stn", None),
        P("chan", "stn", None, None),
        P(),
    )
    return jax.shard_map(
        body, mesh=mesh, in_specs=placed, out_specs=P(None, ("stn", "chan"), None), check_vma=False
    )
```

profile of v0, /device:TPU:2, one launch (start us, length us, event | category | flops | bytes accessed | tf_op | source)
XLA Modules:
  0.0 876.2 jit_solution(455187938880387183)
XLA Ops:
  7.3 4.5 reduce-window.6
  14.1 8.2 scatter_custom_fusion
  23.0 10.4 %all-to-all-start = ((s32[16,192,1]{1,2,0:T(1,128)}), s32[16,192,1]{1,2,0:T(1,128)S(1)}, u32[]{:S(2)}, u32[]{:S(2)}) async-start(s32[16,192,1]{1,2,0:T(1,128)} %all_to_all.43), calls=%async_computation | async-start | bytes 32768 | tf_op jit(solution)/shard_map/all_to_all | solution.py:123
  36.2 4.9 all-to-all-done
  41.1 3.7 all-to-all-start.2
  44.7 6.8 scatter_custom_fusion.1
  51.6 19.8 %all-to-all-done.2 = bf16[16,64,512]{2,0,1:T(8,128)(2,1)S(1)} async-done(((bf16[16,64,512]{2,0,1:T(8,128)(2,1)}), bf16[16,64,512]{2,0,1:T(8,128)(2,1)S(1)}, u32[]{:S(2)}, u32[]{:S(2)}) %all-to-all-start.2) | async-done | bytes 1048608 | tf_op jit(solution)/shard_map/all_to_all | solution.py:94
  71.3 4.8 all-to-all-start.1
  84.7 185.7 %scatter_fusion = bf16[3072,2,128]{2,1,0:T(2,128)(2,1)} fusion(bf16[3072,2,128]{2,1,0:T(2,128)(2,1)} %broadcast_in_dim.128, s32[2048]{0:T(1024)S(1)} %bitcast.146, bf16[2048,2,128]{2,1,0:T(2,128)(2,1)S(1)} %pad_maximum_fusion), kind=kCustom, calls=%fused_computation.2 | custom fusion | bytes 3153920 | tf_op jit(solution)/shard_map/scatter | solution.py:117
  270.4 7.3 all-to-all-start.3
  278.0 37.6 %all-to-all-done.3 = bf16[3072,2,128]{2,1,0:T(2,128)(2,1)} async-done(((bf16[3072,2,128]{2,1,0:T(2,128)(2,1)}), bf16[3072,2,128]{2,1,0:T(2,128)(2,1)}, u32[]{:S(2)}, u32[]{:S(2)}) %all-to-all-start.3) | async-done | bytes 1572896 | tf_op jit(solution)/shard_map/all_to_all | solution.py:121
  315.6 394.3 %while.13 = (s32[]{:T(128)}, f32[16,2048]{1,0:T(8,128)S(1)}, s32[12]{0:T(128)S(1)}, s32[3072]{0:T(1024)S(1)}, s32[3072,128]{1,0:T(8,128)}, /*index=5*/bf16[2,8]{...) while((s32[]{:T(128)}, f32[16,2048]{1,0:T(8,128)S(1)}, ...), condition=%wide.region_7.8_spmd.clone, body=%wide.region_6.7_spmd.clone.sunk | while | flops 293081088 | bytes 26742172 | solution.py:57
  323.7 3.2 fusion.127
  336.1 7.6 fusion.128
  343.7 3.5 copy.26
  356.5 3.2 fusion.127
  368.9 7.6 fusion.128
  376.6 3.5 copy.26
  389.4 3.2 fusion.127
  401.8 7.6 fusion.128
  409.4 3.5 copy.26
  422.2 3.2 fusion.127
  434.6 7.6 fusion.128
  442.3 3.5 copy.26
  455.1 3.2 fusion.127
  467.5 7.6 fusion.128
  475.1 3.5 copy.26
  487.9 3.2 fusion.127
  500.3 7.6 fusion.128
  507.9 3.5 copy.26
  520.8 3.2 fusion.127
  533.2 7.6 fusion.128
  540.8 3.5 copy.26
  553.6 3.2 fusion.127
  566.0 7.6 fusion.128
  573.6 3.5 copy.26
  586.4 3.2 fusion.127
  598.9 7.6 fusion.128
  606.5 3.5 copy.26
  619.3 3.2 fusion.127
  631.7 7.6 fusion.128
  639.3 3.5 copy.26
  664.5 7.6 fusion.128
  672.2 3.5 copy.26
  685.0 3.2 fusion.127
  697.4 7.6 fusion.128
  705.0 3.5 copy.26
  712.2 150.7 %all-reduce.2.cloned.1.call-done = f32[2,128,128]{2,1,0:T(8,128)} async-done(((f32[2,128,128]{2,1,0:T(8,128)}), f32[2,128,128]{2,1,0:T(8,128)}) %all-reduce.2.cloned.1.call-update) | async-done | bytes 131088 | tf_op jit(solution)/shard_map/psum | solution.py:132
  (127 shorter events, 120.5 us)
Async XLA Ops:
  6.5 38.2 %copy-start = (s32[1,1,2048,128]{3,2,1,0:T(8,128)S(1)}, s32[1,1,2048,128]{3,2,1,0:T(8,128)}, u32[]{:S(2)}) copy-start(s32[1,1,2048,128]{3,2,1,0:T(8,128)} %param.10) | copy-start | bytes 3145732
  23.0 18.1 %all-to-all-start = ((s32[16,192,1]{1,2,0:T(1,128)}), s32[16,192,1]{1,2,0:T(1,128)S(1)}, u32[]{:S(2)}, u32[]{:S(2)}) async-start(s32[16,192,1]{1,2,0:T(1,128)} %all_to_all.43), calls=%async_computation | async-start | bytes 32768 | tf_op jit(solution)/shard_map/all_to_all | solution.py:123
  41.1 30.3 %all-to-all-start.2 = ((bf16[16,64,512]{2,0,1:T(8,128)(2,1)}), bf16[16,64,512]{2,0,1:T(8,128)(2,1)S(1)}, u32[]{:S(2)}, u32[]{:S(2)}) async-start(bf16[16,64,512]{2,0,1:T(8,128)(2,1)} %copy.16), calls=%async_computation.2 | async-start | bytes 2097152 | tf_op jit(solution)/shard_map/all_to_all | solution.py:94
  71.3 199.0 %all-to-all-start.1 = ((s32[16,192,128]{2,1,0:T(8,128)}), s32[16,192,128]{2,1,0:T(8,128)}, u32[]{:S(2)}, u32[]{:S(2)}) async-start(s32[16,192,128]{2,1,0:T(8,128)} %bitcast.8), calls=%async_computation.1 | async-start | bytes 3145728 | tf_op jit(solution)/shard_map/all_to_all | solution.py:122
  82.5 233.0 %copy-start.1 = (bf16[2,8]{1,0:T(2,128)(2,1)S(1)}, bf16[2,8]{1,0:T(2,128)(2,1)}, u32[]{:S(2)}) copy-start(bf16[2,8]{1,0:T(2,128)(2,1)} %param.11) | copy-start | bytes 100
  270.4 45.2 %all-to-all-start.3 = ((bf16[3072,2,128]{2,1,0:T(2,128)(2,1)}), bf16[3072,2,128]{2,1,0:T(2,128)(2,1)}, u32[]{:S(2)}, u32[]{:S(2)}) async-start(bf16[3072,2,128]{2,1,0:T(2,128)(2,1)} %scatter_fusion), calls=%async_computation.3 | async-start | bytes 3145728 | tf_op jit(solution)/shard_map/all_to_all | solution.py:121
  277.6 585.3 %all-reduce.2.cloned.1.call-start = ((), (), s32[]{:S(2)}) async-start(), calls=%async_computation.4 | async-start | bytes 262144 | tf_op jit(solution)/shard_map/psum | solution.py:132
Sparse Core Ops, SparseCore 0:
  711.7 151.1 all-reduce.1
where the time goes:
time: 881 us; the launch traced here: 876 us
  local copies, waits for them, and re-layouts  271 us (31%)
  waiting for transfers between devices  213 us (24%)
  loops' own time  128 us (15%)
  other arithmetic  114 us (13%)
  matrix products  111 us (13%)
  starting transfers between devices  26.4 us (3%)
  between operations  13.6 us (2%)
    scatter x1, local copies, waits for them, and re-layouts, body(): jnp.zeros((facets * capacity, 2, VB), jnp.bfloat16).at[slot_ids]  186 us
    psum x1, waiting for transfers between devices, body(): summed = lax.psum(grid, 'chan')  151 us
    another operation x1, loops' own time, grid_blocks(): lax.scan(accumulate, start_grids, jnp.arange(slot_count // group_size))  128 us
    dot_general x12, matrix products, block_tiles(): jnp.einsum('nux,nwx->nuw', along_u, weighted, preferred_element_type=jnp....  91.5 us
    dot_general x12, local copies, waits for them, and re-layouts, block_tiles(): jnp.einsum('nux,nwx->nuw', along_u, weighted, preferred_element_type=jnp....  42.5 us
    convert_element_type x12, other arithmetic, block_tiles(): along_v[:, None, :, :].astype(jnp.float32)  38.9 us
    convert_element_type x12, other arithmetic, block_tiles(): weighted = (values[:, :, None, :].astype(jnp.float32) * along_v[:, None,...  38.3 us
    all_to_all x1, waiting for transfers between devices, body(): lax.all_to_all(send_values, 'stn', split_axis=0, concat_axis=0, tiled=True)  37.6 us
  transfers between devices with their start and end apart: 5, of which 4 were waited for; matrix products, arithmetic and copies ran while one was open for 23% of the time, Pallas kernels for 0%

commit v1 on v0

--- a/solution.py
+++ b/solution.py
@@ -10,6 +10,22 @@
 TS = 4
 TT = 16
 OFFS = 25
+
+
+def pairwise_exchange(array, axis, split, join):
+    ways, here = (lax.axis_size(axis), lax.axis_index(axis))
+    width = array.shape[split] // ways
+    dims = list(array.shape)
+    dims[split] = width
+    height = dims[join]
+    dims[join] = height * ways
+    full = jnp.zeros(dims, array.dtype)
+    for mask in range(ways):
+        part = lax.dynamic_slice_in_dim(array, (here ^ mask) * width, width, axis=split)
+        if mask:
+            part = lax.ppermute(part, axis, [(d, d ^ mask) for d in range(ways)])
+        full = lax.dynamic_update_slice_in_dim(full, part, (here ^ mask) * height, axis=join)
+    return full
 
 
 def kernel_rows(offsets, taps_row):
@@ -118,7 +134,7 @@
     send_offsets = jnp.zeros((facets * capacity, VB), jnp.int32).at[slot_ids].set(offsets)
     send_tiles = jnp.zeros((facets * capacity,), jnp.int32).at[slot_ids].set(tile_ids)
     got_values, got_offsets, got_tiles = (
-        lax.all_to_all(send_values, "stn", split_axis=0, concat_axis=0, tiled=True),
+        pairwise_exchange(send_values, "stn", 0, 0),
         lax.all_to_all(send_offsets, "stn", split_axis=0, concat_axis=0, tiled=True),
         lax.all_to_all(send_tiles, "stn", split_axis=0, concat_axis=0, tiled=True),
     )

time: 881 us -> 839 us (0.952)
  local copies, waits for them, and re-layouts: 271 us -> 217 us
  starting transfers between devices: 26.4 us -> 76.1 us
  waiting for transfers between devices: 213 us -> 168 us
    scatter x1, local copies, waits for them, and re-layouts: 186 us -> 118 us  [body(): jnp.zeros((facets * capacity, 2, VB), jnp.bfloat16).at[slot_ids]]
    ppermute x0 -> x15, starting transfers between devices: none -> 54.2 us  [pairwise_exchange(): part = lax.ppermute(part, axis, [(d, d ^ mask) for d in range(ways)])]
    all_to_all x1 -> x0, waiting for transfers between devices: 37.6 us -> none  [body(): lax.all_to_all(send_values, 'stn', split_axis=0, concat_axis=0, tiled=True)]
    dynamic_update_slice x0 -> x15, local copies, waits for them, and re-layouts: none -> 10.7 us  [pairwise_exchange(): lax.dynamic_update_slice_in_dim(full, part, (here ^ mask) * height, axis=...]
  transfers between devices with their start and end apart: 5 -> 19, of which waited for: 4 -> 5; matrix products, arithmetic and copies ran while one was open for 23% -> 20% of each run, Pallas kernels for 0% -> 0%
where the time goes in v1:
time: 839 us; the launch traced here: 829 us
  local copies, waits for them, and re-layouts  217 us (26%)
  waiting for transfers between devices  168 us (20%)
  loops' own time  131 us (16%)
  other arithmetic  112 us (13%)
  matrix products  111 us (13%)
  starting transfers between devices  76.1 us (9%)
  between operations  13.9 us (2%)
    psum x1, waiting for transfers between devices, body(): summed = lax.psum(grid, 'chan')  151 us
    another operation x1, loops' own time, grid_blocks(): lax.scan(accumulate, start_grids, jnp.arange(slot_count // group_size))  131 us
    scatter x1, local copies, waits for them, and re-layouts, body(): jnp.zeros((facets * capacity, 2, VB), jnp.bfloat16).at[slot_ids]  118 us
    dot_general x12, matrix products, block_tiles(): jnp.einsum('nux,nwx->nuw', along_u, weighted, preferred_element_type=jnp....  91.6 us
    ppermute x15, starting transfers between devices, pairwise_exchange(): part = lax.ppermute(part, axis, [(d, d ^ mask) for d in range(ways)])  54.2 us
    dot_general x12, local copies, waits for them, and re-layouts, block_tiles(): jnp.einsum('nux,nwx->nuw', along_u, weighted, preferred_element_type=jnp....  42.5 us
    convert_element_type x12, other arithmetic, block_tiles(): along_v[:, None, :, :].astype(jnp.float32)  38.9 us
    convert_element_type x12, other arithmetic, block_tiles(): weighted = (values[:, :, None, :].astype(jnp.float32) * along_v[:, None,...  38.6 us
  transfers between devices with their start and end apart: 19, of which 5 were waited for; matrix products, arithmetic and copies ran while one was open for 20% of the time, Pallas kernels for 0%

profile of v1, /device:TPU:2, one launch (start us, length us, event | category | flops | bytes accessed | tf_op | source)
XLA Modules:
  0.0 829.3 jit_solution(5838611937350696184)
XLA Ops:
  9.4 10.4 %all-to-all-start.2 = ((bf16[16,64,512]{2,0,1:T(8,128)(2,1)}), bf16[16,64,512]{2,0,1:T(8,128)(2,1)S(1)}, u32[]{:S(2)}, u32[]{:S(2)}) async-start(bf16[16,64,512]{2,0,1:T(8,128)(2,1)} %copy.16), calls=%async_computation.2 | async-start | bytes 2097152 | tf_op jit(solution)/shard_map/all_to_all | solution.py:110
  19.9 4.5 reduce-window.6
  25.2 8.2 scatter_custom_fusion
  34.2 12.4 %all-to-all-done.2 = bf16[16,64,512]{2,0,1:T(8,128)(2,1)S(1)} async-done(((bf16[16,64,512]{2,0,1:T(8,128)(2,1)}), bf16[16,64,512]{2,0,1:T(8,128)(2,1)S(1)}, u32[]{:S(2)}, u32[]{:S(2)}) %all-to-all-start.2) | async-done | bytes 1048608 | tf_op jit(solution)/shard_map/all_to_all | solution.py:110
  46.5 4.8 all-to-all-start
  51.4 6.8 scatter_custom_fusion.1
  58.9 6.7 all-to-all-start.1
  67.8 3.3 stack_reshape.9
  75.2 117.7 %scatter_fusion = bf16[3072,2,128]{2,1,0:T(2,128)(2,1)S(1)} fusion(bf16[3072,2,128]{2,1,0:T(2,128)(2,1)S(1)} %broadcast.315.clone, s32[2048]{0:T(1024)S(1)} %bitcast.146, bf16[2048,2,128]{2,1,0:T(2,128)(2,1)} %pad_maximum_fusion), kind=kCustom, calls=%fused_computation.2 | custom fusion | bytes 3153920 | tf_op jit(solution)/shard_map/scatter | solution.py:133
  199.4 3.6 collective-permute-start.1
  204.9 4.5 collective-permute-start.3
  211.4 5.4 collective-permute-start.5
  220.2 7.5 collective-permute-start.7
  231.1 4.8 collective-permute-start.9
  236.6 3.7 collective-permute-start.10
  241.0 3.9 collective-permute-start.11
  245.7 3.8 collective-permute-start.12
  250.2 4.8 collective-permute-start.13
  262.1 3.7 collective-permute-done.14
  266.5 396.7 %while.13 = (s32[]{:T(128)}, f32[16,2048]{1,0:T(8,128)S(1)}, s32[12]{0:T(128)S(1)}, s32[3072]{0:T(1024)S(1)}, s32[3072,128]{1,0:T(8,128)}, /*index=5*/bf16[2,8]{...) while((s32[]{:T(128)}, f32[16,2048]{1,0:T(8,128)S(1)}, ...), condition=%wide.region_7.8_spmd.clone, body=%wide.region_6.7_spmd.clone.sunk | while | flops 293081088 | bytes 26742172 | solution.py:73
  274.7 3.2 fusion.119
  287.2 7.6 fusion.120
  294.9 3.5 copy.26
  307.7 3.2 fusion.119
  320.3 7.6 fusion.120
  327.9 3.5 copy.26
  353.3 7.6 fusion.120
  361.0 3.5 copy.26
  373.8 3.2 fusion.119
  386.4 7.6 fusion.120
  394.0 3.5 copy.26
  419.4 7.6 fusion.120
  427.0 3.5 copy.26
  452.4 7.6 fusion.120
  460.1 3.5 copy.26
  485.5 7.6 fusion.120
  493.1 3.5 copy.26
  518.5 7.6 fusion.120
  526.2 3.5 copy.26
  551.6 7.6 fusion.120
  559.2 3.5 copy.26
  584.6 7.6 fusion.120
  592.3 3.5 copy.26
  617.7 7.6 fusion.120
  625.3 3.5 copy.26
  650.7 7.6 fusion.120
  658.3 3.5 copy.26
  665.5 150.5 %all-reduce.2.cloned.1.call-done = f32[2,128,128]{2,1,0:T(8,128)} async-done(((f32[2,128,128]{2,1,0:T(8,128)}), f32[2,128,128]{2,1,0:T(8,128)}) %all-reduce.2.cloned.1.call-update) | async-done | bytes 131088 | tf_op jit(solution)/shard_map/psum | solution.py:148
  (176 shorter events, 169.7 us)
Async XLA Ops:
  6.5 44.9 %copy-start = (s32[1,1,2048,128]{3,2,1,0:T(8,128)S(1)}, s32[1,1,2048,128]{3,2,1,0:T(8,128)}, u32[]{:S(2)}) copy-start(s32[1,1,2048,128]{3,2,1,0:T(8,128)} %param.10) | copy-start | bytes 3145732
  6.5 13.3 %copy-start.3 = (s32[1,1,2048,1]{2,3,1,0:T(1,128)S(1)}, s32[1,1,2048,1]{2,3,1,0:T(1,128)}, u32[]{:S(2)}) copy-start(s32[1,1,2048,1]{2,3,1,0:T(1,128)} %param.8) | copy-start | bytes 24580
  9.4 37.1 %all-to-all-start.2 = ((bf16[16,64,512]{2,0,1:T(8,128)(2,1)}), bf16[16,64,512]{2,0,1:T(8,128)(2,1)S(1)}, u32[]{:S(2)}, u32[]{:S(2)}) async-start(bf16[16,64,512]{2,0,1:T(8,128)(2,1)} %copy.16), calls=%async_computation.2 | async-start | bytes 2097152 | tf_op jit(solution)/shard_map/all_to_all | solution.py:110
  46.5 12.4 %all-to-all-start = ((s32[16,192,1]{1,2,0:T(1,128)}), s32[16,192,1]{1,2,0:T(1,128)S(1)}, u32[]{:S(2)}, u32[]{:S(2)}) async-start(s32[16,192,1]{1,2,0:T(1,128)} %all_to_all.39), calls=%async_computation | async-start | bytes 32768 | tf_op jit(solution)/shard_map/all_to_all | solution.py:139
  58.9 207.6 %all-to-all-start.1 = ((s32[16,192,128]{2,1,0:T(8,128)}), s32[16,192,128]{2,1,0:T(8,128)}, u32[]{:S(2)}, u32[]{:S(2)}) async-start(s32[16,192,128]{2,1,0:T(8,128)} %bitcast.8), calls=%async_computation.1 | async-start | bytes 3145728 | tf_op jit(solution)/shard_map/all_to_all | solution.py:138
  65.7 750.4 %all-reduce.2.cloned.1.call-start = ((), (), s32[]{:S(2)}) async-start(), calls=%async_computation.3 | async-start | bytes 262144 | tf_op jit(solution)/shard_map/psum | solution.py:148
  192.9 73.6 %copy-start.1 = (bf16[2,8]{1,0:T(2,128)(2,1)S(1)}, bf16[2,8]{1,0:T(2,128)(2,1)}, u32[]{:S(2)}) copy-start(bf16[2,8]{1,0:T(2,128)(2,1)} %param.11) | copy-start | bytes 100
  195.8 1.1 copy-start.2
  197.0 14.4 %collective-permute-start = (bf16[192,2,128]{2,1,0:T(2,128)(2,1)}, bf16[192,2,128]{2,1,0:T(2,128)(2,1)S(1)}, u32[]{:S(2)}, u32[]{:S(2)}) collective-permute-start(bf16[192,2,128]{2,1,0:T(2,128)(2,1)} %get-tuple-element.184), channel_id=1, source_target_pairs={{0,32},{32,0},{64,96},{96,64},{128,160},{160,128},{192,224},{224,1... | collective-permute-start | bytes 294920 | tf_op jit(solution)/shard_map/ppermute | solution.py:26
  199.4 18.2 %collective-permute-start.1 = (bf16[192,2,128]{2,1,0:T(2,128)(2,1)}, bf16[192,2,128]{2,1,0:T(2,128)(2,1)S(1)}, u32[]{:S(2)}, u32[]{:S(2)}) collective-permute-start(bf16[192,2,128]{2,1,0:T(2,128)(2,1)} %get-tuple-element.183), channel_id=1, source_target_pairs={{0,64},{32,96},{64,0},{96,32},{128,192},{160,224},{192,128},{224,1... | collective-permute-start | bytes 294920 | tf_op jit(solution)/shard_map/ppermute | solution.py:26
  202.9 17.2 %collective-permute-start.2 = (bf16[192,2,128]{2,1,0:T(2,128)(2,1)}, bf16[192,2,128]{2,1,0:T(2,128)(2,1)S(1)}, u32[]{:S(2)}, u32[]{:S(2)}) collective-permute-start(bf16[192,2,128]{2,1,0:T(2,128)(2,1)} %get-tuple-element.182), channel_id=1, source_target_pairs={{0,96},{32,64},{64,32},{96,0},{128,224},{160,192},{192,160},{224,1... | collective-permute-start | bytes 294920 | tf_op jit(solution)/shard_map/ppermute | solution.py:26
  204.9 23.5 %collective-permute-start.3 = (bf16[192,2,128]{2,1,0:T(2,128)(2,1)}, bf16[192,2,128]{2,1,0:T(2,128)(2,1)S(1)}, u32[]{:S(2)}, u32[]{:S(2)}) collective-permute-start(bf16[192,2,128]{2,1,0:T(2,128)(2,1)} %get-tuple-element.181), channel_id=1, source_target_pairs={{0,128},{32,160},{64,192},{96,224},{128,0},{160,32},{192,64},{224,... | collective-permute-start | bytes 294920 | tf_op jit(solution)/shard_map/ppermute | solution.py:26
  209.4 21.7 %collective-permute-start.4 = (bf16[192,2,128]{2,1,0:T(2,128)(2,1)}, bf16[192,2,128]{2,1,0:T(2,128)(2,1)S(1)}, u32[]{:S(2)}, u32[]{:S(2)}) collective-permute-start(bf16[192,2,128]{2,1,0:T(2,128)(2,1)} %get-tuple-element.180), channel_id=1, source_target_pairs={{0,160},{32,128},{64,224},{96,192},{128,32},{160,0},{192,96},{224,... | collective-permute-start | bytes 294920 | tf_op jit(solution)/shard_map/ppermute | solution.py:26
  211.4 25.2 %collective-permute-start.5 = (bf16[192,2,128]{2,1,0:T(2,128)(2,1)}, bf16[192,2,128]{2,1,0:T(2,128)(2,1)S(1)}, u32[]{:S(2)}, u32[]{:S(2)}) collective-permute-start(bf16[192,2,128]{2,1,0:T(2,128)(2,1)} %get-tuple-element.179), channel_id=1, source_target_pairs={{0,192},{32,224},{64,128},{96,160},{128,64},{160,96},{192,0},{224,... | collective-permute-start | bytes 294920 | tf_op jit(solution)/shard_map/ppermute | solution.py:26
  217.5 23.5 %collective-permute-start.6 = (bf16[192,2,128]{2,1,0:T(2,128)(2,1)S(1)}, bf16[192,2,128]{2,1,0:T(2,128)(2,1)S(1)}, u32[]{:S(2)}, u32[]{:S(2)}) collective-permute-start(bf16[192,2,128]{2,1,0:T(2,128)(2,1)S(1)} %get-tuple-element.178), channel_id=1, source_target_pairs={{0,224},{32,192},{64,160},{96,128},{128,96},{160,64},{192,32},{224... | collective-permute-start | bytes 294920 | tf_op jit(solution)/shard_map/ppermute | solution.py:26
  220.2 25.5 %collective-permute-start.7 = (bf16[192,2,128]{2,1,0:T(2,128)(2,1)S(1)}, bf16[192,2,128]{2,1,0:T(2,128)(2,1)S(1)}, u32[]{:S(2)}, u32[]{:S(2)}) collective-permute-start(bf16[192,2,128]{2,1,0:T(2,128)(2,1)S(1)} %get-tuple-element.177), channel_id=1, source_target_pairs={{0,256},{32,288},{64,320},{96,352},{128,384},{160,416},{192,448},{... | collective-permute-start | bytes 294920 | tf_op jit(solution)/shard_map/ppermute | solution.py:26
  228.4 21.9 %collective-permute-start.8 = (bf16[192,2,128]{2,1,0:T(2,128)(2,1)S(1)}, bf16[192,2,128]{2,1,0:T(2,128)(2,1)S(1)}, u32[]{:S(2)}, u32[]{:S(2)}) collective-permute-start(bf16[192,2,128]{2,1,0:T(2,128)(2,1)S(1)} %get-tuple-element.176), channel_id=1, source_target_pairs={{0,288},{32,256},{64,352},{96,320},{128,416},{160,384},{192,480},{... | collective-permute-start | bytes 294920 | tf_op jit(solution)/shard_map/ppermute | solution.py:26
  231.1 24.6 %collective-permute-start.9 = (bf16[192,2,128]{2,1,0:T(2,128)(2,1)S(1)}, bf16[192,2,128]{2,1,0:T(2,128)(2,1)S(1)}, u32[]{:S(2)}, u32[]{:S(2)}) collective-permute-start(bf16[192,2,128]{2,1,0:T(2,128)(2,1)S(1)} %get-tuple-element.175), channel_id=1, source_target_pairs={{0,320},{32,352},{64,256},{96,288},{128,448},{160,480},{192,384},{... | collective-permute-start | bytes 294920 | tf_op jit(solution)/shard_map/ppermute | solution.py:26
  236.6 22.0 %collective-permute-start.10 = (bf16[192,2,128]{2,1,0:T(2,128)(2,1)S(1)}, bf16[192,2,128]{2,1,0:T(2,128)(2,1)S(1)}, u32[]{:S(2)}, u32[]{:S(2)}) collective-permute-start(bf16[192,2,128]{2,1,0:T(2,128)(2,1)S(1)} %get-tuple-element.174), channel_id=1, source_target_pairs={{0,352},{32,320},{64,288},{96,256},{128,480},{160,448},{192,416},{... | collective-permute-start | bytes 294920 | tf_op jit(solution)/shard_map/ppermute | solution.py:26
  241.0 18.2 %collective-permute-start.11 = (bf16[192,2,128]{2,1,0:T(2,128)(2,1)S(1)}, bf16[192,2,128]{2,1,0:T(2,128)(2,1)S(1)}, u32[]{:S(2)}, u32[]{:S(2)}) collective-permute-start(bf16[192,2,128]{2,1,0:T(2,128)(2,1)S(1)} %get-tuple-element.173), channel_id=1, source_target_pairs={{0,384},{32,416},{64,448},{96,480},{128,256},{160,288},{192,320},{... | collective-permute-start | bytes 294920 | tf_op jit(solution)/shard_map/ppermute | solution.py:26
  245.7 14.3 %collective-permute-start.12 = (bf16[192,2,128]{2,1,0:T(2,128)(2,1)S(1)}, bf16[192,2,128]{2,1,0:T(2,128)(2,1)S(1)}, u32[]{:S(2)}, u32[]{:S(2)}) collective-permute-start(bf16[192,2,128]{2,1,0:T(2,128)(2,1)S(1)} %get-tuple-element.172), channel_id=1, source_target_pairs={{0,416},{32,384},{64,480},{96,448},{128,288},{160,256},{192,352},{... | collective-permute-start | bytes 294920 | tf_op jit(solution)/shard_map/ppermute | solution.py:26
  250.2 11.1 %collective-permute-start.13 = (bf16[192,2,128]{2,1,0:T(2,128)(2,1)S(1)}, bf16[192,2,128]{2,1,0:T(2,128)(2,1)S(1)}, u32[]{:S(2)}, u32[]{:S(2)}) collective-permute-start(bf16[192,2,128]{2,1,0:T(2,128)(2,1)S(1)} %get-tuple-element.171), channel_id=1, source_target_pairs={{0,448},{32,480},{64,384},{96,416},{128,320},{160,352},{192,256},{... | collective-permute-start | bytes 294920 | tf_op jit(solution)/shard_map/ppermute | solution.py:26
  255.7 10.1 %collective-permute-start.14 = (bf16[192,2,128]{2,1,0:T(2,128)(2,1)S(1)}, bf16[192,2,128]{2,1,0:T(2,128)(2,1)S(1)}, u32[]{:S(2)}, u32[]{:S(2)}) collective-permute-start(bf16[192,2,128]{2,1,0:T(2,128)(2,1)S(1)} %get-tuple-element.170), channel_id=1, source_target_pairs={{0,480},{32,448},{64,416},{96,384},{128,352},{160,320},{192,288},{... | collective-permute-start | bytes 294920 | tf_op jit(solution)/shard_map/ppermute | solution.py:26
Sparse Core Ops, SparseCore 0:
  665.1 150.8 all-reduce.1
